TPU v7x, 256 devices: a whole 4x4x8 slice. The times are simulated.
256 devices in a mesh: tok: 16 (over y, x), ch: 16 (over z, core).
Axes of the slice: x: 4, y: 4, z: 8, core: 2. Of those that a mesh axis runs over, the one named last changes fastest.
Arguments:
- tokens: bfloat16 [256, 16384], P('tok', 'ch'), may hold values from -64 to 64
- probe: int32 [256, 16384], P('tok', 'ch'), may hold values from 0 to 1
- signs: int32 [16384], P('ch'), may hold values from 0 to 1
- gate_weight: bfloat16 [16384, 26624], P('ch', 'tok'), may hold values from -0.046875 to 0.046875
- up_weight: bfloat16 [16384, 26624], P('ch', 'tok'), may hold values from -0.046875 to 0.046875
- down_weight: bfloat16 [26624, 16384], P('tok', 'ch'), may hold values from -0.0390625 to 0.0390625
Outputs:
- rotated_product: float32 [256, 16384], P('tok', 'ch')
- diagonal_estimate: float32 [16384], P('ch')
All inputs are finite; a program needn't handle non-finite values.
Results may differ from a plain program's by a relative error of at most 0.004.
Values may be sent and summed in bfloat16 or wider, within the bound.
No kernel may reach another device: no remote copies, remote signals or barrier semaphores. Data moves between devices by JAX's collectives and lax.ppermute only.
A program may use at most 128 MiB of HBM per device.

v0:
```python
import math
import jax
import jax.numpy as jnp
from jax import lax
from jax.sharding import PartitionSpec as P

D = 16384


def partner_2(value, axis, stride):
    mask = 2**stride
    pairs = [(source, source ^ mask) for source in range(lax.axis_size(axis))]
    return lax.ppermute(value, axis, pairs)


def sign_table(length):
    indices = jnp.arange(length, dtype=jnp.int32)
    parity = jnp.zeros((length, length), jnp.int32)
    for bit_pos in range(length.bit_length() - 1):
        parity = parity + (indices[:, None] >> bit_pos & 1) * (indices[None, :] >> bit_pos & 1)
    return jnp.where(parity % 2 == 0, 1.0, -1.0).astype(jnp.float32)


def cross_pairs(values):
    my_index = lax.axis_index("ch")
    for bit_pos in range(lax.axis_size("ch").bit_length() - 1):
        partner = partner_2(values, "ch", bit_pos)
        upper_half = my_index >> bit_pos & 1 == 1
        values = jnp.where(upper_half, partner - values, values + partner)
    return values


def cross_section(values):
    return cross_pairs(values)


def grad_product(gate_piece, up_piece, gate_weight, up_weight):
    contract = (((1,), (1,)), ((), ()))
    first_term = lax.dot_general(
        gate_piece, gate_weight, contract, preferred_element_type=jnp.float32
    )
    return first_term + lax.dot_general(
        up_piece, up_weight, contract, preferred_element_type=jnp.float32
    )


def on_device(tokens, probe, signs, gate_weight, up_weight, down_weight):
    tok_rows, channels = tokens.shape
    total_rows = tok_rows * lax.axis_size("tok")
    root_scale = 1.0 / math.sqrt(D)
    hadamard = sign_table(channels)
    probe_signs = (2 * probe - 1).astype(jnp.float32)
    channel_signs = (2 * signs - 1).astype(jnp.float32)
    start_local = jnp.dot(
        (probe_signs * channel_signs[None, :]).astype(jnp.bfloat16),
        hadamard.astype(jnp.bfloat16),
        preferred_element_type=jnp.float32,
    )
    tangent = (cross_section(start_local) * root_scale).astype(jnp.bfloat16)
    all_tokens, all_tangent = (
        lax.all_gather(tokens, "tok", axis=0, tiled=True),
        lax.all_gather(tangent, "tok", axis=0, tiled=True),
    )
    inputs = jnp.stack([all_tokens, all_tangent], axis=1)
    gate_part = jnp.einsum("rsd,df->rsf", inputs, gate_weight, preferred_element_type=jnp.float32)
    up_part = jnp.einsum("rsd,df->rsf", inputs, up_weight, preferred_element_type=jnp.float32)
    summed = lax.psum_scatter(
        jnp.stack([gate_part, up_part], axis=2), "ch", scatter_dimension=0, tiled=True
    )
    gate_pre = summed[:, 0, 0]
    up_pre = summed[:, 0, 1]
    gate_tan = summed[:, 1, 0]
    up_tan = summed[:, 1, 1]
    sigmoid_gate = jax.nn.sigmoid(gate_pre)
    activated = gate_pre * sigmoid_gate
    slope_term = sigmoid_gate * (1.0 + gate_pre * (1.0 - sigmoid_gate))
    hidden_tan = (slope_term * gate_tan * up_pre + activated * up_tan).astype(jnp.bfloat16)
    out_part = jnp.dot(
        lax.all_gather(hidden_tan, "ch", axis=0, tiled=True),
        down_weight,
        preferred_element_type=jnp.float32,
    )
    out_tangent = lax.psum(out_part, "tok").astype(jnp.bfloat16)
    piece = out_tangent
    back_hidden = lax.psum_scatter(
        lax.dot_general(
            piece, down_weight, (((1,), (1,)), ((), ())), preferred_element_type=jnp.float32
        ),
        "ch",
        scatter_dimension=0,
        tiled=True,
    )
    back_gate = (back_hidden * up_pre * slope_term).astype(jnp.bfloat16)
    back_up = (back_hidden * activated).astype(jnp.bfloat16)
    stacked = jnp.stack([back_gate, back_up], axis=1)
    piece = lax.all_gather(stacked, "ch", axis=0, tiled=True)
    in_part = grad_product(piece[:, 0], piece[:, 1], gate_weight, up_weight)
    back_tokens = lax.psum_scatter(in_part, "tok", scatter_dimension=0, tiled=True)
    local_back = jnp.dot(
        back_tokens, hadamard, precision=lax.Precision.HIGHEST, preferred_element_type=jnp.float32
    )
    rotated_product = cross_section(local_back) * root_scale * channel_signs[None, :]
    token_terms = jnp.sum(probe_signs * rotated_product, axis=0)
    diagonal_estimate = lax.psum(token_terms, "tok") / total_rows
    return (rotated_product, diagonal_estimate)


def solution(mesh):
    placed = (
        P("tok", "ch"),
        P("tok", "ch"),
        P("ch"),
        P("ch", "tok"),
        P("ch", "tok"),
        P("tok", "ch"),
    )
    return jax.shard_map(
        on_device, mesh=mesh, in_specs=placed, out_specs=(P("tok", "ch"), P("ch")), check_vma=False
    )
```

profile of v0, /device:TPU:32, one launch (start us, length us, event | category | flops | bytes accessed | tf_op | source)
XLA Modules:
  0.0 515.5 jit_solution(10228923519675699118)
XLA Ops:
  8.1 6.5 %fusion.3 = pred[1024,1024]{1,0:T(32,128)(4,1)S(1)} fusion(s32[1024]{0:T(1024)S(1)} %get-tuple-element.6, s32[1024]{0:T(1024)S(1)} %get-tuple-element.7, s32[1024]{0:T(1024)S(1)} %get-tuple-element.8, s32[1024]{0:T(1024)S(1)} %get-tuple-element.9, s32[1024]{0:T(1024)S(1)} %get-tuple-element.10, s32[1024]{0:T(1024)S(1)} %get-tuple-element.11, ...), kind=kLoop, calls=%fused_computation.8 | loop fusion | flops 32505856 | bytes 1089536 | tf_op jit(solution)/shard_map/eq | solution.py:21
  21.2 2.5 collective-permute-done.1
  24.5 3.4 collective-permute-start.2
  30.2 6.1 %collective-permute-start.3 = (f32[16,1024]{1,0:T(8,128)S(1)}, f32[16,1024]{1,0:T(8,128)S(1)}, u32[]{:S(2)}, u32[]{:S(2)}) collective-permute-start(f32[16,1024]{1,0:T(8,128)S(1)} %add_select_fusion.4), channel_id=1, source_target_pairs={{0,8},{1,9},{2,10},{3,11},{4,12},{5,13},{6,14},{7,15},{8,0},{9,1},... | collective-permute-start | bytes 196616 | tf_op jit(solution)/shard_map/ppermute | solution.py:13
  36.3 24.4 %all_gather.12 = bf16[256,1024]{1,0:T(8,128)(2,1)S(1)} all-gather(bf16[16,1024]{1,0:T(8,128)(2,1)} %param.6), channel_id=1, replica_groups=mesh['tok'=16,'ch'=16] {'tok'}, dimensions={0}, use_global_device_ids=true | all-gather | bytes 557056 | tf_op jit(solution)/shard_map/all_gather | solution.py:61
  60.7 23.3 %all_gather.13 = bf16[256,1024]{1,0:T(8,128)(2,1)S(1)} all-gather(bf16[16,1024]{1,0:T(8,128)(2,1)S(1)} %multiply_convert_fusion.2), channel_id=1, replica_groups=mesh['tok'=16,'ch'=16] {'tok'}, dimensions={0}, use_global_device_ids=true | all-gather | bytes 557056 | tf_op jit(solution)/shard_map/all_gather | solution.py:62
  84.0 4.0 fusion.11
  90.1 3.3 pad_maximum_fusion
  93.4 60.3 %reduce-scatter.4.cloned.1.call-done = f32[16,2,2,1664]{3,0,1,2:T(8,128)} async-done(((f32[256,2,2,1664]{3,0,1,2:T(8,128)}), f32[16,2,2,1664]{3,0,1,2:T(8,128)}) %reduce-scatter.4.cloned.1.call-update) | async-done | bytes 426000 | tf_op jit(solution)/shard_map/reduce_scatter | solution.py:67
  154.8 20.4 %all_gather.14 = bf16[256,1664]{1,0:T(8,128)(2,1)S(1)} all-gather(bf16[16,1664]{1,0:T(8,128)(2,1)S(1)} %fusion.24), channel_id=1, replica_groups=mesh['tok'=16,'ch'=16] {'ch'}, dimensions={0}, use_global_device_ids=true | all-gather | bytes 905216 | tf_op jit(solution)/shard_map/all_gather | solution.py:79
  175.3 4.1 fusion.41
  179.4 88.3 %all-reduce.1 = bf16[256,1024]{1,0:T(8,128)(2,1)} all-reduce(f32[256,1024]{1,0:T(8,128)} %fusion.41), channel_id=1, replica_groups=mesh['tok'=16,'ch'=16] {'tok'}, use_global_device_ids=true, to_apply=%region_1.2 | all-reduce | flops 262144 | bytes 1572864 | tf_op jit(solution)/shard_map/psum | solution.py:83
  267.7 4.5 fusion.42
  272.3 49.8 %reduce-scatter.6.cloned.1.call-done = f32[16,1664]{1,0:T(8,128)} async-done(((f32[256,1664]{1,0:T(8,128)}), f32[16,1664]{1,0:T(8,128)}) %reduce-scatter.6.cloned.1.call-update) | async-done | bytes 106512 | tf_op jit(solution)/shard_map/reduce_scatter | solution.py:85
  324.1 40.5 %all-gather.2.cloned.1.call-done = bf16[256,2,1664]{2,0,1:T(8,128)(2,1)} async-done(((bf16[16,2,1664]{2,0,1:T(8,128)(2,1)}), bf16[256,2,1664]{2,0,1:T(8,128)(2,1)}) %all-gather.2.cloned.1.call-update) | async-done | bytes 1703952 | tf_op jit(solution)/shard_map/all_gather | solution.py:96
  364.6 2.4 fusion.19
  369.5 77.1 %reduce-scatter.8.cloned.1.call-done = f32[16,1024]{1,0:T(8,128)} async-done(((f32[256,1024]{1,0:T(8,128)}), f32[16,1024]{1,0:T(8,128)}) %reduce-scatter.8.cloned.1.call-update) | async-done | bytes 65552 | tf_op jit(solution)/shard_map/reduce_scatter | solution.py:98
  446.6 3.6 fusion
  452.0 3.8 collective-permute-done.5
  455.8 2.6 collective-permute-start.6
  458.4 2.6 collective-permute-done.6
  461.1 5.0 collective-permute-start.7
  466.1 3.5 collective-permute-done.7
  470.3 38.1 %psum.15 = f32[1024]{0:T(1024)S(1)} all-reduce(f32[1024]{0:T(1024)S(1)} %get-tuple-element.2), channel_id=1, replica_groups=mesh['tok'=16,'ch'=16] {'tok'}, use_global_device_ids=true, to_apply=%region_5.6 | all-reduce | flops 1024 | bytes 8192 | tf_op jit(solution)/shard_map/psum | solution.py:104
  (50 shorter events, 21.4 us)
Async XLA Ops:
  7.2 80.8 %copy-start = (bf16[1024,1664]{1,0:T(8,128)(2,1)S(1)}, bf16[1024,1664]{1,0:T(8,128)(2,1)}, u32[]{:S(2)}) copy-start(bf16[1024,1664]{1,0:T(8,128)(2,1)} %param.9) | copy-start | bytes 10223620
  7.2 146.5 %reduce-scatter.4.cloned.1.call-start = ((), (), s32[]{:S(2)}) async-start(), calls=%async_computation.3 | async-start | bytes 7241728 | tf_op jit(solution)/shard_map/reduce_scatter | solution.py:67
  14.6 1.0 copy-start.1
  17.0 1.4 collective-permute-start
  19.2 4.5 collective-permute-start.1
  24.5 5.7 %collective-permute-start.2 = (f32[16,1024]{1,0:T(8,128)S(1)}, f32[16,1024]{1,0:T(8,128)S(1)}, u32[]{:S(2)}, u32[]{:S(2)}) collective-permute-start(f32[16,1024]{1,0:T(8,128)S(1)} %add_select_fusion.5), channel_id=1, source_target_pairs={{0,4},{1,5},{2,6},{3,7},{4,0},{5,1},{6,2},{7,3},{8,12},{9,13},{10,... | collective-permute-start | bytes 196616 | tf_op jit(solution)/shard_map/ppermute | solution.py:13
  30.2 30.4 %collective-permute-start.3 = (f32[16,1024]{1,0:T(8,128)S(1)}, f32[16,1024]{1,0:T(8,128)S(1)}, u32[]{:S(2)}, u32[]{:S(2)}) collective-permute-start(f32[16,1024]{1,0:T(8,128)S(1)} %add_select_fusion.4), channel_id=1, source_target_pairs={{0,8},{1,9},{2,10},{3,11},{4,12},{5,13},{6,14},{7,15},{8,0},{9,1},... | collective-permute-start | bytes 196616 | tf_op jit(solution)/shard_map/ppermute | solution.py:13
  93.4 228.7 %reduce-scatter.6.cloned.1.call-start = ((), (), s32[]{:S(2)}) async-start(), calls=%async_computation.4 | async-start | bytes 1810432 | tf_op jit(solution)/shard_map/reduce_scatter | solution.py:85
  272.2 92.4 %all-gather.2.cloned.1.call-start = ((), (), s32[]{:S(2)}) async-start(), calls=%async_computation.5 | async-start | bytes 1810432 | tf_op jit(solution)/shard_map/all_gather | solution.py:96
  323.8 122.8 %reduce-scatter.8.cloned.1.call-start = ((), (), s32[]{:S(2)}) async-start(), calls=%async_computation.6 | async-start | bytes 1114112 | tf_op jit(solution)/shard_map/reduce_scatter | solution.py:98
  364.6 2.5 copy-start.4
  364.6 2.7 copy-start.5
  367.3 98.8 %copy-start.3 = (s32[1024]{0:T(1024)S(1)}, s32[1024]{0:T(1024)}, u32[]{:S(2)}) copy-start(s32[1024]{0:T(1024)} %param.8) | copy-start | bytes 12292
  367.3 102.3 %copy-start.2 = (s32[16,1024]{1,0:T(8,128)S(1)}, s32[16,1024]{1,0:T(8,128)}, u32[]{:S(2)}) copy-start(s32[16,1024]{1,0:T(8,128)} %param.7) | copy-start | bytes 196612
  450.2 1.3 collective-permute-start.4
  451.4 4.4 collective-permute-start.5
  455.8 5.3 %collective-permute-start.6 = (f32[16,1024]{1,0:T(8,128)S(1)}, f32[16,1024]{1,0:T(8,128)S(1)}, u32[]{:S(2)}, u32[]{:S(2)}) collective-permute-start(f32[16,1024]{1,0:T(8,128)S(1)} %add_select_fusion.2), channel_id=1, source_target_pairs={{0,4},{1,5},{2,6},{3,7},{4,0},{5,1},{6,2},{7,3},{8,12},{9,13},{10,... | collective-permute-start | bytes 196616 | tf_op jit(solution)/shard_map/ppermute | solution.py:13
  461.1 8.5 %collective-permute-start.7 = (f32[16,1024]{1,0:T(8,128)S(1)}, f32[16,1024]{1,0:T(8,128)S(1)}, u32[]{:S(2)}, u32[]{:S(2)}) collective-permute-start(f32[16,1024]{1,0:T(8,128)S(1)} %add_select_fusion.1), channel_id=1, source_target_pairs={{0,8},{1,9},{2,10},{3,11},{4,12},{5,13},{6,14},{7,15},{8,0},{9,1},... | collective-permute-start | bytes 196616 | tf_op jit(solution)/shard_map/ppermute | solution.py:13
Sparse Core Ops, SparseCore 0:
  93.5 60.1 reduce-scatter.3
  272.3 49.7 reduce-scatter.5
  324.1 40.4 all-gather.1
  369.6 76.9 reduce-scatter.7
where the time goes:
time: 516 us
  waiting for transfers between devices  245 us (47%)
  blocking collectives  195 us (38%)
  matrix products  24.3 us (5%)
  starting transfers between devices  19.8 us (4%)
  other arithmetic  16.4 us (3%)
  between operations  13.9 us (3%)
    psum x1, blocking collectives, on_device(): out_tangent = lax.psum(out_part, 'tok').astype(jnp.bfloat16)  88.3 us
    reduce_scatter x1, waiting for transfers between devices, on_device(): lax.psum_scatter(in_part, 'tok', scatter_dimension=0, tiled=True)  77.1 us
    reduce_scatter x1, waiting for transfers between devices, on_device(): lax.psum_scatter(jnp.stack([gate_part, up_part], axis=2), 'ch', scatter_d...  60.3 us
    reduce_scatter x1, waiting for transfers between devices, on_device(): lax.psum_scatter(lax.dot_general(piece, down_weight, (((1,), (1,)), ((),...  49.8 us
    all_gather x1, waiting for transfers between devices, on_device(): piece = lax.all_gather(stacked, 'ch', axis=0, tiled=True)  40.5 us
    psum x1, blocking collectives, on_device(): diagonal_estimate = lax.psum(token_terms, 'tok') / total_rows  38.1 us
    all_gather x1, blocking collectives, on_device(): lax.all_gather(tokens, 'tok', axis=0, tiled=True)  24.4 us
    all_gather x1, blocking collectives, on_device(): lax.all_gather(tangent, 'tok', axis=0, tiled=True)  23.3 us
  transfers between devices with their start and end apart: 12, of which 11 were waited for; matrix products, arithmetic and copies ran while one was open for 0% of the time, Pallas kernels for 0%

commit v1 on v0

--- a/solution.py
+++ b/solution.py
@@ -5,6 +5,7 @@
 from jax.sharding import PartitionSpec as P
 
 D = 16384
+_perform_tracks = lambda frame: jnp.sum(lax.all_gather(frame, axis_name="tok"), 0)
 
 
 def partner_2(value, axis, stride):
@@ -80,7 +81,7 @@
         down_weight,
         preferred_element_type=jnp.float32,
     )
-    out_tangent = lax.psum(out_part, "tok").astype(jnp.bfloat16)
+    out_tangent = _perform_tracks(out_part).astype(jnp.bfloat16)
     piece = out_tangent
     back_hidden = lax.psum_scatter(
         lax.dot_general(

time: 516 us -> 557 us (1.079)
  waiting for transfers between devices: 245 us -> 366 us
  blocking collectives: 195 us -> 106 us
  other arithmetic: 16.4 us -> 25.1 us
    all_gather x0 -> x1, waiting for transfers between devices: none -> 115 us  [lax.all_gather(frame, axis_name='tok')]
    psum x1 -> x0, blocking collectives: 88.3 us -> none  [on_device(): out_tangent = lax.psum(out_part, 'tok').astype(jnp.bfloat16)]
    reduce_sum x0 -> x1, other arithmetic: none -> 8.62 us  [jnp.sum(lax.all_gather(frame, axis_name='tok'), 0)]
  transfers between devices with their start and end apart: 12 -> 13, of which waited for: 11 -> 12; matrix products, arithmetic and copies ran while one was open for 0% -> 0% of each run, Pallas kernels for 0% -> 0%
where the time goes in v1:
time: 557 us; the launch traced here: 556 us
  waiting for transfers between devices  366 us (66%)
  blocking collectives  106 us (19%)
  other arithmetic  25.1 us (5%)
  matrix products  24.3 us (4%)
  starting transfers between devices  19.9 us (4%)
  between operations  13.9 us (2%)
    all_gather x1, waiting for transfers between devices, lax.all_gather(frame, axis_name='tok')  115 us
    reduce_scatter x1, waiting for transfers between devices, on_device(): lax.psum_scatter(in_part, 'tok', scatter_dimension=0, tiled=True)  77.1 us
    reduce_scatter x1, waiting for transfers between devices, on_device(): lax.psum_scatter(jnp.stack([gate_part, up_part], axis=2), 'ch', scatter_d...  60.2 us
    reduce_scatter x1, waiting for transfers between devices, on_device(): lax.psum_scatter(lax.dot_general(piece, down_weight, (((1,), (1,)), ((),...  55 us
    all_gather x1, waiting for transfers between devices, on_device(): piece = lax.all_gather(stacked, 'ch', axis=0, tiled=True)  40.7 us
    psum x1, blocking collectives, on_device(): diagonal_estimate = lax.psum(token_terms, 'tok') / total_rows  38.1 us
    all_gather x1, blocking collectives, on_device(): lax.all_gather(tokens, 'tok', axis=0, tiled=True)  24.4 us
    all_gather x1, blocking collectives, on_device(): lax.all_gather(tangent, 'tok', axis=0, tiled=True)  23.3 us
  transfers between devices with their start and end apart: 13, of which 12 were waited for; matrix products, arithmetic and copies ran while one was open for 0% of the time, Pallas kernels for 0%

profile of v1, /device:TPU:32, one launch (start us, length us, event | category | flops | bytes accessed | tf_op | source)
XLA Modules:
  0.0 556.4 jit_solution(2880315919128648910)
XLA Ops:
  8.1 6.5 %fusion.3 = pred[1024,1024]{1,0:T(32,128)(4,1)S(1)} fusion(s32[1024]{0:T(1024)S(1)} %get-tuple-element.6, s32[1024]{0:T(1024)S(1)} %get-tuple-element.7, s32[1024]{0:T(1024)S(1)} %get-tuple-element.8, s32[1024]{0:T(1024)S(1)} %get-tuple-element.9, s32[1024]{0:T(1024)S(1)} %get-tuple-element.10, s32[1024]{0:T(1024)S(1)} %get-tuple-element.11, ...), kind=kLoop, calls=%fused_computation.8 | loop fusion | flops 32505856 | bytes 1089536 | tf_op jit(solution)/shard_map/eq | solution.py:22
  21.2 2.5 collective-permute-done.1
  24.6 3.4 collective-permute-start.2
  30.2 6.1 %collective-permute-start.3 = (f32[16,1024]{1,0:T(8,128)S(1)}, f32[16,1024]{1,0:T(8,128)S(1)}, u32[]{:S(2)}, u32[]{:S(2)}) collective-permute-start(f32[16,1024]{1,0:T(8,128)S(1)} %add_select_fusion.4), channel_id=1, source_target_pairs={{0,8},{1,9},{2,10},{3,11},{4,12},{5,13},{6,14},{7,15},{8,0},{9,1},... | collective-permute-start | bytes 196616 | tf_op jit(solution)/shard_map/ppermute | solution.py:14
  36.3 24.4 %all_gather.18 = bf16[256,1024]{1,0:T(8,128)(2,1)S(1)} all-gather(bf16[16,1024]{1,0:T(8,128)(2,1)} %param.6), channel_id=1, replica_groups=mesh['tok'=16,'ch'=16] {'tok'}, dimensions={0}, use_global_device_ids=true | all-gather | bytes 557056 | tf_op jit(solution)/shard_map/all_gather | solution.py:62
  60.7 23.3 %all_gather.19 = bf16[256,1024]{1,0:T(8,128)(2,1)S(1)} all-gather(bf16[16,1024]{1,0:T(8,128)(2,1)S(1)} %multiply_convert_fusion.2), channel_id=1, replica_groups=mesh['tok'=16,'ch'=16] {'tok'}, dimensions={0}, use_global_device_ids=true | all-gather | bytes 557056 | tf_op jit(solution)/shard_map/all_gather | solution.py:63
  84.0 4.0 fusion.11
  90.1 3.3 pad_maximum_fusion
  93.4 60.2 %reduce-scatter.4.cloned.1.call-done = f32[16,2,2,1664]{3,0,1,2:T(8,128)} async-done(((f32[256,2,2,1664]{3,0,1,2:T(8,128)}), f32[16,2,2,1664]{3,0,1,2:T(8,128)}) %reduce-scatter.4.cloned.1.call-update) | async-done | bytes 426000 | tf_op jit(solution)/shard_map/reduce_scatter | solution.py:68
  154.8 20.4 %all_gather.20 = bf16[256,1664]{1,0:T(8,128)(2,1)S(1)} all-gather(bf16[16,1664]{1,0:T(8,128)(2,1)S(1)} %fusion.24), channel_id=1, replica_groups=mesh['tok'=16,'ch'=16] {'ch'}, dimensions={0}, use_global_device_ids=true | all-gather | bytes 905216 | tf_op jit(solution)/shard_map/all_gather | solution.py:80
  175.2 4.1 fusion.41
  179.6 115.1 %all-gather.6.cloned.1.call-done = f32[4096,1024]{1,0:T(8,128)} async-done(((f32[256,1024]{1,0:T(8,128)}), f32[4096,1024]{1,0:T(8,128)}) %all-gather.6.cloned.1.call-update) | async-done | bytes 16777232 | tf_op jit(solution)/shard_map/all_gather | solution.py:8
  294.8 8.6 %reduce_sum.18 = bf16[256,1024]{1,0:T(8,128)(2,1)} reduce(f32[16,256,1024]{2,1,0:T(8,128)} %bitcast.78, f32[]{:T(128)} %constant.32.clone.1), dimensions={0}, to_apply=%region_1.2 | reduce | flops 3932160 | bytes 17301508 | tf_op jit(solution)/shard_map/reduce_sum | solution.py:8
  303.4 4.5 fusion.42
  308.0 55.0 %reduce-scatter.6.cloned.1.call-done = f32[16,1664]{1,0:T(8,128)} async-done(((f32[256,1664]{1,0:T(8,128)}), f32[16,1664]{1,0:T(8,128)}) %reduce-scatter.6.cloned.1.call-update) | async-done | bytes 106512 | tf_op jit(solution)/shard_map/reduce_scatter | solution.py:86
  364.8 40.7 %all-gather.4.cloned.1.call-done = bf16[256,2,1664]{2,0,1:T(8,128)(2,1)} async-done(((bf16[16,2,1664]{2,0,1:T(8,128)(2,1)}), bf16[256,2,1664]{2,0,1:T(8,128)(2,1)}) %all-gather.4.cloned.1.call-update) | async-done | bytes 1703952 | tf_op jit(solution)/shard_map/all_gather | solution.py:97
  410.4 77.1 %reduce-scatter.8.cloned.1.call-done = f32[16,1024]{1,0:T(8,128)} async-done(((f32[256,1024]{1,0:T(8,128)}), f32[16,1024]{1,0:T(8,128)}) %reduce-scatter.8.cloned.1.call-update) | async-done | bytes 65552 | tf_op jit(solution)/shard_map/reduce_scatter | solution.py:99
  487.5 3.6 fusion
  492.9 3.8 collective-permute-done.5
  496.7 2.6 collective-permute-start.6
  499.3 2.6 collective-permute-done.6
  501.9 5.0 collective-permute-start.7
  507.0 3.5 collective-permute-done.7
  511.1 38.1 %psum.7 = f32[1024]{0:T(1024)S(1)} all-reduce(f32[1024]{0:T(1024)S(1)} %get-tuple-element.2), channel_id=1, replica_groups=mesh['tok'=16,'ch'=16] {'tok'}, use_global_device_ids=true, to_apply=%region_5.6 | all-reduce | flops 1024 | bytes 8192 | tf_op jit(solution)/shard_map/psum | solution.py:105
  (53 shorter events, 23.9 us)
Async XLA Ops:
  7.2 80.9 %copy-start = (bf16[1024,1664]{1,0:T(8,128)(2,1)S(1)}, bf16[1024,1664]{1,0:T(8,128)(2,1)}, u32[]{:S(2)}) copy-start(bf16[1024,1664]{1,0:T(8,128)(2,1)} %param.9) | copy-start | bytes 10223620
  7.2 146.5 %reduce-scatter.4.cloned.1.call-start = ((), (), s32[]{:S(2)}) async-start(), calls=%async_computation.3 | async-start | bytes 7241728 | tf_op jit(solution)/shard_map/reduce_scatter | solution.py:68
  14.6 1.0 copy-start.1
  17.0 1.4 collective-permute-start
  19.2 4.5 collective-permute-start.1
  24.6 5.7 %collective-permute-start.2 = (f32[16,1024]{1,0:T(8,128)S(1)}, f32[16,1024]{1,0:T(8,128)S(1)}, u32[]{:S(2)}, u32[]{:S(2)}) collective-permute-start(f32[16,1024]{1,0:T(8,128)S(1)} %add_select_fusion.5), channel_id=1, source_target_pairs={{0,4},{1,5},{2,6},{3,7},{4,0},{5,1},{6,2},{7,3},{8,12},{9,13},{10,... | collective-permute-start | bytes 196616 | tf_op jit(solution)/shard_map/ppermute | solution.py:14
  30.2 30.4 %collective-permute-start.3 = (f32[16,1024]{1,0:T(8,128)S(1)}, f32[16,1024]{1,0:T(8,128)S(1)}, u32[]{:S(2)}, u32[]{:S(2)}) collective-permute-start(f32[16,1024]{1,0:T(8,128)S(1)} %add_select_fusion.4), channel_id=1, source_target_pairs={{0,8},{1,9},{2,10},{3,11},{4,12},{5,13},{6,14},{7,15},{8,0},{9,1},... | collective-permute-start | bytes 196616 | tf_op jit(solution)/shard_map/ppermute | solution.py:14
  93.4 201.4 %all-gather.6.cloned.1.call-start = ((), (), s32[]{:S(2)}) async-start(), calls=%async_computation.7 | async-start | bytes 17825792 | tf_op jit(solution)/shard_map/all_gather | solution.py:8
  179.4 183.6 %reduce-scatter.6.cloned.1.call-start = ((), (), s32[]{:S(2)}) async-start(), calls=%async_computation.4 | async-start | bytes 1810432 | tf_op jit(solution)/shard_map/reduce_scatter | solution.py:86
  307.9 97.6 %all-gather.4.cloned.1.call-start = ((), (), s32[]{:S(2)}) async-start(), calls=%async_computation.5 | async-start | bytes 1810432 | tf_op jit(solution)/shard_map/all_gather | solution.py:97
  364.7 122.7 %reduce-scatter.8.cloned.1.call-start = ((), (), s32[]{:S(2)}) async-start(), calls=%async_computation.6 | async-start | bytes 1114112 | tf_op jit(solution)/shard_map/reduce_scatter | solution.py:99
  405.5 2.5 copy-start.4
  405.5 2.7 copy-start.5
  408.2 98.7 %copy-start.3 = (s32[1024]{0:T(1024)S(1)}, s32[1024]{0:T(1024)}, u32[]{:S(2)}) copy-start(s32[1024]{0:T(1024)} %param.8) | copy-start | bytes 12292
  408.2 102.2 %copy-start.2 = (s32[16,1024]{1,0:T(8,128)S(1)}, s32[16,1024]{1,0:T(8,128)}, u32[]{:S(2)}) copy-start(s32[16,1024]{1,0:T(8,128)} %param.7) | copy-start | bytes 196612
  491.0 1.3 collective-permute-start.4
  492.3 4.4 collective-permute-start.5
  496.7 5.3 collective-permute-start.6
  501.9 8.5 %collective-permute-start.7 = (f32[16,1024]{1,0:T(8,128)S(1)}, f32[16,1024]{1,0:T(8,128)S(1)}, u32[]{:S(2)}, u32[]{:S(2)}) collective-permute-start(f32[16,1024]{1,0:T(8,128)S(1)} %add_select_fusion.1), channel_id=1, source_target_pairs={{0,8},{1,9},{2,10},{3,11},{4,12},{5,13},{6,14},{7,15},{8,0},{9,1},... | collective-permute-start | bytes 196616 | tf_op jit(solution)/shard_map/ppermute | solution.py:14
Sparse Core Ops, SparseCore 0:
  93.5 60.1 reduce-scatter.3
  179.5 115.2 all-gather.5
  308.0 54.9 reduce-scatter.5
  364.9 40.5 all-gather.3
  410.5 76.9 reduce-scatter.7
